TPU v7x, 32 devices: a whole 2x2x4 slice. The times are simulated.
32 devices in a mesh: dp: 8 (over z, y), tp: 4 (over x, core).
Axes of the slice: x: 2, y: 2, z: 4, core: 2. Of those that a mesh axis runs over, the one named last changes fastest.
Arguments:
- hidden: bfloat16 [16, 4096], P('dp'), may hold values from -6 to 6
- attention_norm_gain: bfloat16 [4096], replicated, may hold values from 0.5 to 1.5
- query_key_value_weight: bfloat16 [4096, 4, 1280], P('dp', 'tp'), may hold values from -0.09375 to 0.09375
- key_value_cache: bfloat16 [16, 2048, 4, 256], P('dp', None, 'tp'), may hold values from -6 to 6
- cache_fill_lengths: int32 [16], P('dp'), may hold values from 2 to 2048
- output_weight_frozen: bfloat16 [4, 1024, 4096], P('tp', None, 'dp'), may hold values from -0.09375 to 0.09375
- adapter_down_transposed: bfloat16 [64, 4, 1024], P(None, 'tp', 'dp'), may hold values from -0.09375 to 0.09375
- adapter_up_matrix: bfloat16 [64, 4, 1024], P(None, 'tp', 'dp'), may hold values from -0.75 to 0.75
- attention_rows: bfloat16 [4096, 4096], P('dp', 'tp'), may hold values from -6 to 6
- upstream: bfloat16 [4096, 4096], P('dp', 'tp'), may hold values from -6 to 6
- rewards: float32 [16], P('dp'), may hold values from 0 to 2
- prompt_group_index: int32 [16], P('dp'), may hold values from 0 to 3, as said below
- completion_live_lengths: int32 [16], P('dp'), may hold values from 1 to 256
Outputs:
- decoded: float32 [16, 4096], P('dp')
- adapted_output_rows: float32 [4096, 4096], P('dp', 'tp')
- grad_lora_a_t: float32 [64, 4, 1024], P(None, 'tp', 'dp')
- grad_lora_b: float32 [64, 4, 1024], P(None, 'tp', 'dp')
Inputs may be any that keep to these rules, and one draw needn't show every extreme that they name: `prompt_group_index`: each prompt holds exactly 4 rollouts.
All inputs are finite; a program needn't handle non-finite values.
Results may differ from a plain program's by a relative error of at most 0.0041.
Values may be sent and summed in bfloat16 or wider, within the bound.
A program may use at most 128 MiB of HBM per device.

v0:
```python
import math

import jax
import jax.numpy as jnp
from jax import lax
from jax.sharding import PartitionSpec as P

HD = 128
HEADS_TP = 8
GROUP = 4
COMP = 256


adapter_scale = 2.0


def rms_norm(decode_state, gain):
    scale = lax.rsqrt(jnp.mean(decode_state * decode_state, axis=-1, keepdims=True) + 1e-05)
    return decode_state * scale * gain.astype(jnp.float32)


def attend(query, cache, lengths, new_keys, new_values):
    head = query.shape[-1]
    slots = cache.shape[1]
    factor = 1.0 / math.sqrt(head)
    keys = cache[:, :, :head].astype(jnp.float32)
    values = cache[:, :, head:]
    scores = jnp.einsum("bhd,bcd->bhc", query, keys, precision=lax.Precision.HIGHEST) * factor
    valid = jnp.arange(slots, dtype=jnp.int32)[None, None, :] < lengths[:, None, None]
    scores = jnp.where(valid, scores, -1e30)
    extra = jnp.einsum("bhd,bed->bhe", query, new_keys, precision=lax.Precision.HIGHEST) * factor
    joined = jnp.concatenate([scores, extra], axis=-1)
    top = jnp.max(joined, axis=-1, keepdims=True)
    expo = jnp.exp(joined - top)
    probs = (expo / jnp.sum(expo, axis=-1, keepdims=True)).astype(jnp.bfloat16)
    out = jnp.einsum("bhc,bcd->bhd", probs[..., :slots], values, preferred_element_type=jnp.float32)
    out = out + jnp.einsum(
        "bhe,bed->bhd",
        probs[..., slots:].astype(jnp.float32),
        new_values,
        precision=lax.Precision.HIGHEST,
    )
    return out.astype(jnp.bfloat16).reshape(query.shape[0], -1)


def shards(
    hidden,
    attention_norm_gain,
    query_key_value_weight,
    key_value_cache,
    cache_fill_lengths,
    output_weight_frozen,
    adapter_down_transposed,
    adapter_up_matrix,
    attention_rows,
    upstream,
    rewards,
    prompt_group_index,
    completion_live_lengths,
):
    a_piece, b_piece = (
        lax.all_gather(adapter_down_transposed, "dp", axis=2, tiled=True),
        lax.all_gather(adapter_up_matrix, "dp", axis=2, tiled=True),
    )
    b_whole = lax.all_gather(b_piece, "tp", axis=1, tiled=True)
    up_matrix_flat = b_whole.reshape(b_whole.shape[0], -1).astype(jnp.float32)
    a_local = a_piece[:, 0, :]
    up_matrix_columns = b_piece[:, 0, :]
    w_rows = query_key_value_weight[:, 0, :].astype(jnp.float32)
    w_cols = output_weight_frozen[0]
    query_width = HEADS_TP * HD
    local_rolls = hidden.shape[0]
    decode_state = hidden.astype(jnp.float32)
    keys_new = []
    values_new = []
    for step in range(2):
        normed = rms_norm(decode_state, attention_norm_gain)
        spread = lax.all_to_all(normed, "dp", split_axis=1, concat_axis=0, tiled=True)
        partial_value = jnp.dot(spread, w_rows, precision=lax.Precision.HIGHEST)
        qkv = lax.psum_scatter(partial_value, "dp", scatter_dimension=0, tiled=True)
        query = qkv[:, :query_width].reshape(local_rolls, HEADS_TP, HD)
        keys_new.append(qkv[:, query_width : query_width + HD])
        values_new.append(qkv[:, query_width + HD :])
        attended = attend(
            query,
            key_value_cache[:, :, 0, :],
            cache_fill_lengths,
            jnp.stack(keys_new, axis=1),
            jnp.stack(values_new, axis=1),
        )
        columns = jnp.dot(
            lax.all_gather(attended, "dp", axis=0, tiled=True),
            w_cols,
            preferred_element_type=jnp.float32,
        )
        returned_values = lax.all_to_all(columns, "dp", split_axis=0, concat_axis=1, tiled=True)
        low_rank_decode = jnp.dot(attended, a_local.T, preferred_element_type=jnp.float32)
        state_update = returned_values + adapter_scale * jnp.dot(
            low_rank_decode, up_matrix_flat, precision=lax.Precision.HIGHEST
        )
        decode_state = decode_state + lax.psum(state_update, "tp")
    groups = local_rolls * lax.axis_size("dp") // GROUP
    onehot = (prompt_group_index[:, None] == jnp.arange(groups, dtype=jnp.int32)[None, :]).astype(
        jnp.float32
    )
    totals, squares = lax.psum(
        (
            jnp.sum(onehot * rewards[:, None], axis=0),
            jnp.sum(onehot * (rewards * rewards)[:, None], axis=0),
        ),
        "dp",
    )
    mean = totals / GROUP
    std = jnp.sqrt(jnp.maximum(squares / GROUP - mean * mean, 0.09))
    advantage = (rewards - jnp.sum(onehot * mean[None, :], axis=1)) / jnp.sum(
        onehot * std[None, :], axis=1
    )
    per_roll = advantage / completion_live_lengths.astype(jnp.float32)
    rows = attention_rows.shape[0]
    slot = jnp.arange(rows, dtype=jnp.int32) % COMP
    limit = jnp.repeat(completion_live_lengths, COMP)
    row_w = jnp.where(slot < limit, jnp.repeat(per_roll, COMP), 0.0)
    whole_rows = jnp.dot(
        attention_rows,
        lax.all_gather(output_weight_frozen, "dp", axis=2, tiled=True)[0],
        preferred_element_type=jnp.float32,
    )
    frozen_output_rows = lax.psum_scatter(whole_rows, "tp", scatter_dimension=1, tiled=True)
    low_sum = lax.psum(jnp.dot(attention_rows, a_local.T, preferred_element_type=jnp.float32), "tp")
    low_rank_rows = low_sum.astype(jnp.bfloat16)
    adapted_output_rows = frozen_output_rows + adapter_scale * jnp.dot(
        low_rank_rows, up_matrix_columns, preferred_element_type=jnp.float32
    )
    advantage_weighted = (row_w[:, None] * upstream.astype(jnp.float32)).astype(jnp.bfloat16)
    backward_result = lax.psum(
        jnp.dot(advantage_weighted, up_matrix_columns.T, preferred_element_type=jnp.float32), "tp"
    ).astype(jnp.bfloat16)
    down_gradient = adapter_scale * lax.dot_general(
        backward_result,
        attention_rows,
        (((0,), (0,)), ((), ())),
        preferred_element_type=jnp.float32,
    )
    up_gradient = adapter_scale * lax.dot_general(
        low_rank_rows,
        advantage_weighted,
        (((0,), (0,)), ((), ())),
        preferred_element_type=jnp.float32,
    )
    grad_a_part, grad_b_part = (
        lax.psum_scatter(down_gradient[:, None, :], "dp", scatter_dimension=2, tiled=True),
        lax.psum_scatter(up_gradient[:, None, :], "dp", scatter_dimension=2, tiled=True),
    )
    return (decode_state, adapted_output_rows, grad_a_part, grad_b_part)


def solution(mesh):
    placed = (
        P("dp", None),
        P(),
        P("dp", "tp", None),
        P("dp", None, "tp", None),
        P("dp"),
        P("tp", None, "dp"),
        P(None, "tp", "dp"),
        P(None, "tp", "dp"),
        P("dp", "tp"),
        P("dp", "tp"),
        P("dp"),
        P("dp"),
        P("dp"),
    )
    return jax.shard_map(
        shards,
        mesh=mesh,
        in_specs=placed,
        out_specs=(P("dp", None), P("dp", "tp"), P(None, "tp", "dp"), P(None, "tp", "dp")),
        check_vma=False,
    )
```

profile of v0, /device:TPU:0, one launch (start us, length us, event | category | flops | bytes accessed | tf_op | source)
XLA Modules:
  0.0 510.0 jit_solution(1464161154151364458)
XLA Ops:
  9.7 13.8 %all_to_all.70 = f32[2,8,512]{2,0,1:T(2,128)S(1)} all-to-all(f32[2,8,512]{2,0,1:T(2,128)S(1)} %bitcast.114), channel_id=1, replica_groups=mesh['dp'=8,'tp'=4] {'dp'}, dimensions={1} | all-to-all | bytes 65536 | tf_op jit(solution)/shard_map/all_to_all | solution.py:78
  23.6 1.3 fusion.8
  25.6 26.2 %all_gather.20 = bf16[64,1,1024]{2,0,1:T(8,128)(2,1)S(1)} all-gather(bf16[64,1,128]{2,0,1:T(8,128)(2,1)S(1)} %copy-done.4), channel_id=1, replica_groups=mesh['dp'=8,'tp'=4] {'dp'}, dimensions={2}, use_global_device_ids=true | all-gather | bytes 147456 | tf_op jit(solution)/shard_map/all_gather | solution.py:63
  51.9 7.2 %all_gather.21 = bf16[64,4,1024]{2,0,1:T(8,128)(2,1)S(1)} all-gather(bf16[64,1,1024]{2,0,1:T(8,128)(2,1)S(1)} %all_gather.20), channel_id=1, replica_groups=mesh['dp'=8,'tp'=4] {'tp'}, dimensions={1}, use_global_device_ids=true | all-gather | bytes 655360 | tf_op jit(solution)/shard_map/all_gather | solution.py:65
  60.4 26.2 %all_gather.19 = bf16[64,1,1024]{2,0,1:T(8,128)(2,1)S(1)} all-gather(bf16[64,1,128]{2,0,1:T(8,128)(2,1)S(1)} %copy-done.5), channel_id=1, replica_groups=mesh['dp'=8,'tp'=4] {'dp'}, dimensions={2}, use_global_device_ids=true | all-gather | bytes 147456 | tf_op jit(solution)/shard_map/all_gather | solution.py:62
  86.6 5.3 %all-reduce.8.cloned.1.call-done = f32[16,1280]{1,0:T(8,128)} async-done(((f32[16,1280]{1,0:T(8,128)}), f32[16,1280]{1,0:T(8,128)}) %all-reduce.8.cloned.1.call-update) | async-done | bytes 81936
  93.7 2.2 fusion.75
  96.4 1.5 fusion.12
  97.9 31.7 %all-gather = bf16[8,2,1024]{2,1,0:T(2,128)(2,1)S(1)} all-gather(bf16[1,2,1024]{2,1,0:T(2,128)(2,1)S(1)} %reshape.138), channel_id=1, replica_groups=mesh['dp'=8,'tp'=4] {'dp'}, dimensions={0}, use_global_device_ids=true | all-gather | bytes 36864 | tf_op jit(solution)/shard_map/all_gather | solution.py:92
  130.5 4.1 all-to-all-start.1
  134.7 6.7 %all-to-all-done.1 = f32[8,2,512]{2,1,0:T(2,128)S(1)} async-done(((f32[8,2,512]{2,1,0:T(2,128)}), f32[8,2,512]{2,1,0:T(2,128)S(1)}, u32[]{:S(2)}, u32[]{:S(2)}) %all-to-all-start.1) | async-done | bytes 32800 | tf_op jit(solution)/shard_map/all_to_all | solution.py:96
  141.7 10.3 %psum.42 = f32[2,4096]{1,0:T(2,128)S(1)} all-reduce(f32[2,4096]{1,0:T(2,128)S(1)} %fusion.3), channel_id=1, replica_groups=mesh['dp'=8,'tp'=4] {'tp'}, use_global_device_ids=true, to_apply=%region_4.5 | all-reduce | flops 8192 | bytes 65536 | tf_op jit(solution)/shard_map/psum | solution.py:101
  152.3 12.2 %all_to_all.71 = f32[2,8,512]{2,0,1:T(2,128)S(1)} all-to-all(f32[2,8,512]{2,0,1:T(2,128)S(1)} %bitcast.113), channel_id=1, replica_groups=mesh['dp'=8,'tp'=4] {'dp'}, dimensions={1} | all-to-all | bytes 65536 | tf_op jit(solution)/shard_map/all_to_all | solution.py:78
  164.5 1.3 fusion.6
  165.8 56.4 %all-gather.4.cloned.1.call-done = bf16[1,1024,4096]{2,1,0:T(8,128)(2,1)} async-done(((bf16[1,1024,512]{2,1,0:T(8,128)(2,1)}), bf16[1,1024,4096]{2,1,0:T(8,128)(2,1)}) %all-gather.4.cloned.1.call-update) | async-done | bytes 8388624 | tf_op jit(solution)/shard_map/all_gather | solution.py:125
  222.2 11.4 %fusion = f32[512,4096]{1,0:T(8,128)} fusion(bf16[512,1024]{1,0:T(8,128)(2,1)} %param.21, bf16[1,1024,4096]{2,1,0:T(8,128)(2,1)} %all-gather.4.cloned.1.call-done), kind=kOutput, calls=%fused_computation | convolution fusion | flops 4294967296 | bytes 17825792 | tf_op jit(solution)/shard_map/dot_general | solution.py:123
  234.4 18.1 %all-reduce.2 = (f32[4]{0:T(128)S(1)}, f32[4]{0:T(128)S(1)}) all-reduce(f32[4]{0:T(128)S(1)} %get-tuple-element.22, f32[4]{0:T(128)S(1)} %get-tuple-element.23), channel_id=1, replica_groups=mesh['dp'=8,'tp'=4] {'dp'}, use_global_device_ids=true, to_apply=%region_14.15 | all-reduce | flops 8 | bytes 64 | tf_op jit(solution)/shard_map/psum | solution.py:106
  252.9 1.7 fusion.23
  254.7 1.7 fusion.28
  256.3 37.2 %all-reduce.10.cloned.1.call-done = f32[16,1280]{1,0:T(8,128)} async-done(((f32[16,1280]{1,0:T(8,128)}), f32[16,1280]{1,0:T(8,128)}) %all-reduce.10.cloned.1.call-update) | async-done | bytes 81936
  295.3 2.2 fusion.76
  297.9 1.5 fusion.18
  299.5 30.6 %all-gather.1 = bf16[8,2,1024]{2,1,0:T(2,128)(2,1)S(1)} all-gather(bf16[1,2,1024]{2,1,0:T(2,128)(2,1)S(1)} %reshape.140), channel_id=1, replica_groups=mesh['dp'=8,'tp'=4] {'dp'}, dimensions={0}, use_global_device_ids=true | all-gather | bytes 36864 | tf_op jit(solution)/shard_map/all_gather | solution.py:92
  331.0 4.3 all-to-all-start.3
  335.5 6.5 %all-to-all-done.3 = f32[8,2,512]{2,1,0:T(2,128)S(1)} async-done(((f32[8,2,512]{2,1,0:T(2,128)}), f32[8,2,512]{2,1,0:T(2,128)S(1)}, u32[]{:S(2)}, u32[]{:S(2)}) %all-to-all-start.3) | async-done | bytes 32800 | tf_op jit(solution)/shard_map/all_to_all | solution.py:96
  342.3 20.3 %all-reduce.11 = (f32[2,4096]{1,0:T(2,128)S(1)}, bf16[512,64]{0,1:T(8,128)(2,1)S(1)}, bf16[512,64]{0,1:T(8,128)(2,1)S(1)}) all-reduce(f32[2,4096]{1,0:T(2,128)S(1)} %fusion.2, f32[512,64]{0,1:T(8,128)S(1)} %fusion.28, f32[512,64]{0,1:T(8,128)S(1)} %fusion.23), channel_id=1, replica_groups=mesh['dp'=8,'tp'=4] {'tp'}, use_global_device_ids=true, to_apply=%region_10.11 | all-reduce | flops 73728 | bytes 458752 | tf_op jit(solution)/shard_map/psum | solution.py:101
  362.6 2.4 fusion.10
  365.1 1.0 fusion.11
  366.8 4.9 reduce-scatter.4.cloned.1.call-done
  371.7 3.4 multiply_add_fusion
  375.0 62.9 %reduce-scatter.8.cloned.1.call-done = f32[64,1,128]{2,0,1:T(8,128)} async-done(((f32[64,1,1024]{2,0,1:T(8,128)}), f32[64,1,128]{2,0,1:T(8,128)}) %reduce-scatter.8.cloned.1.call-update) | async-done | bytes 32784 | tf_op jit(solution)/shard_map/reduce_scatter | solution.py:152
  437.9 65.3 %reduce-scatter.6.cloned.1.call-done = f32[64,1,128]{2,0,1:T(8,128)} async-done(((f32[64,1,1024]{2,0,1:T(8,128)}), f32[64,1,128]{2,0,1:T(8,128)}) %reduce-scatter.6.cloned.1.call-update) | async-done | bytes 32784 | tf_op jit(solution)/shard_map/reduce_scatter | solution.py:151
  (82 shorter events, 13.5 us)
Async XLA Ops:
  7.2 16.4 %copy-start = (bf16[512,1,1280]{2,0,1:T(8,128)(2,1)S(1)}, bf16[512,1,1280]{2,0,1:T(8,128)(2,1)}, u32[]{:S(2)}) copy-start(bf16[512,1,1280]{2,0,1:T(8,128)(2,1)} %param.15) | copy-start | bytes 3932164
  7.2 18.4 %copy-start.4 = (bf16[64,1,128]{2,0,1:T(8,128)(2,1)S(1)}, bf16[64,1,128]{2,0,1:T(8,128)(2,1)}, u32[]{:S(2)}) copy-start(bf16[64,1,128]{2,0,1:T(8,128)(2,1)} %param.20) | copy-start | bytes 49156
  7.2 84.8 %all-reduce.8.cloned.1.call-start = ((), (), s32[]{:S(2)}) async-start(), calls=%async_computation.11 | async-start | bytes 163840
  23.5 35.6 %copy-start.10 = (u32[32]{0:T(128)S(1)}, u32[32]{0:T(128)}, u32[]{:S(2)}) copy-start(u32[32]{0:T(128)} %constant.58) | copy-start | bytes 388
  23.6 36.8 %copy-start.5 = (bf16[64,1,128]{2,0,1:T(8,128)(2,1)S(1)}, bf16[64,1,128]{2,0,1:T(8,128)(2,1)}, u32[]{:S(2)}) copy-start(bf16[64,1,128]{2,0,1:T(8,128)(2,1)} %param.19) | copy-start | bytes 49156
  23.6 63.0 %copy-start.9 = (s32[2]{0:T(128)S(1)}, s32[2]{0:T(128)}, u32[]{:S(2)}) copy-start(s32[2]{0:T(128)} %param.17) | copy-start | bytes 28
  24.9 197.4 %all-gather.4.cloned.1.call-start = ((), (), s32[]{:S(2)}) async-start(), calls=%async_computation.7 | async-start | bytes 9437184 | tf_op jit(solution)/shard_map/all_gather | solution.py:125
  59.0 70.5 %copy-start.1 = (bf16[1,1024,512]{2,1,0:T(8,128)(2,1)S(1)}, bf16[1,1024,512]{2,1,0:T(8,128)(2,1)}, u32[]{:S(2)}) copy-start(bf16[1,1024,512]{2,1,0:T(8,128)(2,1)} %param.18) | copy-start | bytes 3145732
  93.7 58.3 %copy-start.3 = (bf16[2,4096]{1,0:T(2,128)(2,1)S(1)}, bf16[2,4096]{1,0:T(2,128)(2,1)}, u32[]{:S(2)}) copy-start(bf16[2,4096]{1,0:T(2,128)(2,1)} %param.13) | copy-start | bytes 49156
  130.5 10.9 %all-to-all-start.1 = ((f32[8,2,512]{2,1,0:T(2,128)}), f32[8,2,512]{2,1,0:T(2,128)S(1)}, u32[]{:S(2)}, u32[]{:S(2)}) async-start(f32[8,2,512]{2,1,0:T(2,128)} %copy.53), calls=%async_computation.1 | async-start | bytes 65536 | tf_op jit(solution)/shard_map/all_to_all | solution.py:96
  134.5 159.0 %all-reduce.10.cloned.1.call-start = ((), (), s32[]{:S(2)}) async-start(), calls=%async_computation.12 | async-start | bytes 163840
  165.8 205.9 %reduce-scatter.4.cloned.1.call-start = ((), (), s32[]{:S(2)}) async-start(), calls=%async_computation.8 | async-start | bytes 10485760 | tf_op jit(solution)/shard_map/reduce_scatter | solution.py:128
  233.7 0.7 copy-start.7
  233.7 0.7 copy-start.6
  233.7 19.1 %copy-start.8 = (s32[2]{0:T(128)S(1)}, s32[2]{0:T(128)}, u32[]{:S(2)}) copy-start(s32[2]{0:T(128)} %param.25) | copy-start | bytes 28
  330.4 34.7 %copy-start.2 = (bf16[512,1024]{1,0:T(8,128)(2,1)S(1)}, bf16[512,1024]{1,0:T(8,128)(2,1)}, u32[]{:S(2)}) copy-start(bf16[512,1024]{1,0:T(8,128)(2,1)} %param.21) | copy-start | bytes 3145732
  331.0 11.0 %all-to-all-start.3 = ((f32[8,2,512]{2,1,0:T(2,128)}), f32[8,2,512]{2,1,0:T(2,128)S(1)}, u32[]{:S(2)}, u32[]{:S(2)}) async-start(f32[8,2,512]{2,1,0:T(2,128)} %copy.59), calls=%async_computation.3 | async-start | bytes 65536 | tf_op jit(solution)/shard_map/all_to_all | solution.py:96
  335.3 102.6 %reduce-scatter.8.cloned.1.call-start = ((), (), s32[]{:S(2)}) async-start(), calls=%async_computation.10 | async-start | bytes 294912 | tf_op jit(solution)/shard_map/reduce_scatter | solution.py:152
  365.0 138.2 %reduce-scatter.6.cloned.1.call-start = ((), (), s32[]{:S(2)}) async-start(), calls=%async_computation.9 | async-start | bytes 294912 | tf_op jit(solution)/shard_map/reduce_scatter | solution.py:151
Sparse Core Ops, SparseCore 0:
  25.0 66.9 all-reduce.7
  94.0 128.1 all-gather.3
  226.2 67.2 all-reduce.9
  296.0 75.6 reduce-scatter.3
  375.4 62.4 reduce-scatter.7
  441.7 61.4 reduce-scatter.5
where the time goes:
time: 511 us; the launch traced here: 510 us
  waiting for transfers between devices  246 us (48%)
  blocking collectives  197 us (39%)
  matrix products  33.4 us (7%)
  between operations  15 us (3%)
  starting transfers between devices  8.6 us (2%)
  local copies, waits for them, and re-layouts  6.15 us (1%)
    reduce_scatter x1, waiting for transfers between devices, shards(): lax.psum_scatter(down_gradient[:, None, :], 'dp', scatter_dimension=2, ti...  65.3 us
    reduce_scatter x1, waiting for transfers between devices, shards(): lax.psum_scatter(up_gradient[:, None, :], 'dp', scatter_dimension=2, tile...  62.9 us
    all_gather x2, blocking collectives, shards(): lax.all_gather(attended, 'dp', axis=0, tiled=True)  62.3 us
    all_gather x1, waiting for transfers between devices, shards(): lax.all_gather(output_weight_frozen, 'dp', axis=2, tiled=True)[0]  56.4 us
    unnamed x8, waiting for transfers between devices  43.3 us
    psum x2, blocking collectives, shards(): decode_state = decode_state + lax.psum(state_update, 'tp')  30.6 us
    all_gather x1, blocking collectives, shards(): lax.all_gather(adapter_up_matrix, 'dp', axis=2, tiled=True)  26.2 us
    all_gather x1, blocking collectives, shards(): lax.all_gather(adapter_down_transposed, 'dp', axis=2, tiled=True)  26.2 us
  transfers between devices with their start and end apart: 8, of which 8 were waited for; matrix products, arithmetic and copies ran while one was open for 8% of the time, Pallas kernels for 0%

commit v1 on v0

--- a/solution.py
+++ b/solution.py
@@ -3,6 +3,8 @@
 import jax
 import jax.numpy as jnp
 from jax import lax
+from jax.experimental import pallas as pl
+from jax.experimental.pallas import tpu as pltpu
 from jax.sharding import PartitionSpec as P
 
 HD = 128
@@ -41,6 +43,571 @@
         precision=lax.Precision.HIGHEST,
     )
     return out.astype(jnp.bfloat16).reshape(query.shape[0], -1)
+
+
+MESH = pl.DeviceIdType.MESH
+F32 = jnp.float32
+BF16 = jnp.bfloat16
+NT = (((1,), (1,)), ((), ()))
+TN = (((0,), (0,)), ((), ()))
+CHUNK = 256
+
+
+def split3(v):
+    hi = v.astype(BF16)
+    rest = v - hi.astype(F32)
+    mid = rest.astype(BF16)
+    lo = (rest - mid.astype(F32)).astype(BF16)
+    return jnp.concatenate([hi, mid, lo], axis=0)
+
+
+def exact_dot(v, w, dims=(((1,), (0,)), ((), ()))):
+    n = v.shape[0]
+    r = lax.dot_general(split3(v), w, dims, preferred_element_type=F32)
+    return r[:n] + r[n : 2 * n] + r[2 * n :]
+
+
+def rows_of(ref, n):
+    return jnp.concatenate([ref[i] for i in range(n)], axis=0)
+
+
+def lanes_of(ref, n):
+    return jnp.concatenate([ref[i] for i in range(n)], axis=1)
+
+
+def fused_kernel(
+    ndp,
+    ntp,
+    h_ref,
+    gain_ref,
+    wqkv_ref,
+    cache_ref,
+    lens_ref,
+    wo_ref,
+    a_ref,
+    b_ref,
+    x_ref,
+    up_ref,
+    stats_ref,
+    dec_ref,
+    out_ref,
+    ga_ref,
+    gb_ref,
+    hbuf,
+    abuf,
+    bbuf,
+    bdbuf,
+    statbuf,
+    qsend,
+    qrecv,
+    asend,
+    arecv,
+    usend,
+    urecv,
+    fsend,
+    frecv,
+    lbsend,
+    lbrecv,
+    gsend,
+    grecv,
+    wt_ref,
+    xbuf,
+    wbuf,
+    pbuf,
+    prcv,
+    ds_s,
+    ds_r,
+    ts_s,
+    ts_r,
+    bd_s,
+    bd_r,
+    xs_s,
+    xs_r,
+    wl_s,
+    wl_r,
+    wf_s,
+    wf_r,
+    ps_s,
+    ps_r,
+    loc,
+):
+    d = lax.axis_index("dp")
+    t = lax.axis_index("tp")
+    z, y = d // 2, d % 2
+    x, c = t // 2, t % 2
+    nz = ndp // 2
+    rolls = h_ref.shape[1]
+    width = h_ref.shape[2]
+    model = ndp * width
+    rank = a_ref.shape[0]
+    piece = a_ref.shape[1]
+    chunks = wo_ref.shape[1] // CHUNK
+    qkvw = wqkv_ref.shape[1]
+    rows = x_ref.shape[0]
+
+    barrier = pltpu.get_barrier_semaphore()
+    for i in range(ndp):
+        for j in range(ntp):
+            if i or j:
+                pl.semaphore_signal(
+                    barrier,
+                    inc=1,
+                    device_id=((d + i) % ndp, (t + j) % ntp),
+                    device_id_type=MESH,
+                )
+    pl.semaphore_wait(barrier, ndp * ntp - 1)
+
+    sent = []
+
+    def send(src, dst, s, r, dev):
+        cp = pltpu.make_async_remote_copy(
+            src_ref=src, dst_ref=dst, send_sem=s, recv_sem=r, device_id=dev, device_id_type=MESH
+        )
+        return cp
+
+    def dp_start(e, src, dst):
+        for off in range(1, ndp):
+            peer = (d + off) % ndp
+            cp = send(src(peer), dst.at[d], ds_s.at[e, off], ds_r.at[e, off], (peer, t))
+            cp.start()
+            sent.append(cp)
+
+    def dp_wait(e, src, dst):
+        for off in range(1, ndp):
+            frm = (d + ndp - off) % ndp
+            send(src(d), dst.at[frm], ds_s.at[e, off], ds_r.at[e, off], (frm, t)).wait_recv()
+
+    def tp_start(e, src, dst):
+        for off in range(1, ntp):
+            peer = (t + off) % ntp
+            cp = send(src, dst.at[t], ts_s.at[e, off], ts_r.at[e, off], (d, peer))
+            cp.start()
+            sent.append(cp)
+
+    def tp_wait(e, src, dst):
+        for off in range(1, ntp):
+            frm = (t + ntp - off) % ntp
+            send(src, dst.at[frm], ts_s.at[e, off], ts_r.at[e, off], (d, frm)).wait_recv()
+
+    dp_start(0, lambda p: h_ref.at[p], hbuf)
+    hbuf[d] = h_ref[d]
+    dp_start(1, lambda p: a_ref, abuf)
+    abuf[d] = a_ref[...]
+    dp_start(2, lambda p: b_ref, bbuf)
+    bbuf[d] = b_ref[...]
+    dp_start(3, lambda p: stats_ref, statbuf)
+    statbuf[d] = stats_ref[...]
+    per = width // piece
+    half = ndp // per
+    bdst = t * half + d // per
+    bslot = d % per
+    for j in range(ntp):
+        tj = (t + j) % ntp
+        if j == 0:
+            here = bdst == d
+
+            @pl.when(here)
+            def _():
+                bdbuf[bslot] = b_ref[...]
+
+            @pl.when(jnp.logical_not(here))
+            def _():
+                send(b_ref, bdbuf.at[bslot], bd_s.at[0], bd_r.at[bslot], (bdst, tj)).start()
+
+        else:
+            cp = send(b_ref, bdbuf.at[bslot], bd_s.at[j], bd_r.at[bslot], (bdst, tj))
+            cp.start()
+            sent.append(cp)
+    mate = 2 * x + (1 - c)
+    xcp = send(x_ref, xbuf.at[c], xs_s.at[0], xs_r.at[0], (d, mate))
+    xcp.start()
+    sent.append(xcp)
+    xbuf[c] = x_ref[...]
+
+    dp_wait(0, lambda p: h_ref.at[p], hbuf)
+    state = rows_of(hbuf, ndp)
+    gain = gain_ref[d]
+    new_k, new_v = [], []
+    factor = 1.0 / math.sqrt(HD)
+
+    def line_sends(go):
+        for ch in range(chunks):
+            for off in range(nz):
+                zt = (z + off) % nz
+                cp = send(
+                    wo_ref.at[:, pl.ds(ch * CHUNK, CHUNK)],
+                    wbuf.at[z // 2, y, c, ch],
+                    wl_s.at[ch, off],
+                    wl_r.at[z // 2, c, ch],
+                    (2 * zt + y, 2 * x + z % 2),
+                )
+                if off == 0:
+
+                    @pl.when(z % 2 != c)
+                    def _():
+                        if go:
+                            cp.start()
+                        else:
+                            cp.wait_send()
+
+                    if go:
+
+                        @pl.when(z % 2 == c)
+                        def _():
+                            lc = pltpu.make_async_copy(
+                                wo_ref.at[:, pl.ds(ch * CHUNK, CHUNK)],
+                                wbuf.at[z // 2, y, c, ch],
+                                loc.at[ch],
+                            )
+                            lc.start()
+                            lc.wait()
+
+                elif go:
+                    cp.start()
+                else:
+                    cp.wait_send()
+
+    for step in range(2):
+        squares = jnp.sum(state * state, axis=-1, keepdims=True)
+        part = exact_dot(state * gain, wqkv_ref[...])
+        both = jnp.concatenate([part, jnp.broadcast_to(squares, (ndp * rolls, 128))], axis=1)
+        for i in range(ndp):
+            qsend[step, i] = both[i * rolls : (i + 1) * rolls]
+        dp_start(4 + 2 * step, lambda p: qsend.at[step, p], qrecv.at[step])
+        qrecv[step, d] = qsend[step, d]
+        if step == 0:
+            dp_wait(1, lambda p: a_ref, abuf)
+            at = lanes_of(abuf, ndp)
+            dp_wait(2, lambda p: b_ref, bbuf)
+            bt = lanes_of(bbuf, ndp)
+            dp_wait(3, lambda p: stats_ref, statbuf)
+            tot = statbuf[0]
+            for i in range(1, ndp):
+                tot = tot + statbuf[i]
+            mean = tot[0:1] / GROUP
+            std = jnp.sqrt(jnp.maximum(tot[1:2] / GROUP - mean * mean, 0.09))
+            for r in range(rolls):
+                one = stats_ref[2 + r : 3 + r]
+                rew = stats_ref[2 + rolls + r : 3 + rolls + r, 0:1]
+                live = stats_ref[2 + 2 * rolls + r : 3 + 2 * rolls + r, 0:1]
+                adv = (rew - jnp.sum(one * mean, axis=1, keepdims=True)) / jnp.sum(
+                    one * std, axis=1, keepdims=True
+                )
+                slot = lax.broadcasted_iota(jnp.int32, (COMP, 1), 0).astype(F32)
+                row_w = jnp.where(slot < live, adv / live, 0.0)
+                seg = pl.ds(r * COMP, COMP)
+                wt_ref[seg, :] = (row_w * up_ref[seg, :].astype(F32)).astype(BF16)
+            lbsend[0] = lax.dot_general(at, x_ref[...], NT, preferred_element_type=F32)
+            lbsend[1] = lax.dot_general(bt, wt_ref[...], NT, preferred_element_type=F32)
+        dp_wait(4 + 2 * step, lambda p: qsend.at[step, p], qrecv.at[step])
+        total = qrecv[step, 0]
+        for i in range(1, ndp):
+            total = total + qrecv[step, i]
+        qkv = total[:, :qkvw] * lax.rsqrt(total[:, qkvw : qkvw + 1] / model + 1e-05)
+        new_k.append(qkv[:, HEADS_TP * HD : HEADS_TP * HD + HD])
+        new_v.append(qkv[:, HEADS_TP * HD + HD :])
+        for b in range(rolls):
+            q = jnp.concatenate(
+                [qkv[b : b + 1, h * HD : (h + 1) * HD] for h in range(HEADS_TP)], axis=0
+            )
+            scores = exact_dot(q, cache_ref[b, :, :HD], NT) * factor
+            pos = lax.broadcasted_iota(jnp.int32, scores.shape, 1)
+            scores = jnp.where(pos < lens_ref[b], scores, -1e30)
+            extra = [
+                jnp.sum(q * k[b : b + 1], axis=-1, keepdims=True) * factor for k in new_k
+            ]
+            top = jnp.max(scores, axis=-1, keepdims=True)
+            for e in extra:
+                top = jnp.maximum(top, e)
+            expo = jnp.exp(scores - top)
+            ee = [jnp.exp(e - top) for e in extra]
+            den = jnp.sum(expo, axis=-1, keepdims=True)
+            for e in ee:
+                den = den + e
+            att = jnp.dot(
+                (expo / den).astype(BF16), cache_ref[b, :, HD:], preferred_element_type=F32
+            )
+            for e, v in zip(ee, new_v):
+                att = att + (e / den).astype(BF16).astype(F32) * v[b : b + 1]
+            att = att.astype(BF16).astype(F32)
+            asend[step, b : b + 1, :] = jnp.concatenate(
+                [att[h : h + 1] for h in range(HEADS_TP)], axis=1
+            )
+        dp_start(5 + 2 * step, lambda p: asend.at[step], arecv.at[step])
+        arecv[step, d] = asend[step]
+        if step == 0:
+            tp_start(2, lbsend, lbrecv)
+            lbrecv[t] = lbsend[...]
+        else:
+            tp_wait(2, lbsend, lbrecv)
+            lb = lbrecv[0]
+            for i in range(1, ntp):
+                lb = lb + lbrecv[i]
+            lb = lb.astype(BF16)
+            low_t, back_t = lb[0], lb[1]
+            ga = adapter_scale * jnp.dot(back_t, x_ref[...], preferred_element_type=F32)
+            gb = adapter_scale * jnp.dot(low_t, wt_ref[...], preferred_element_type=F32)
+            for i in range(ndp):
+                gsend[i, 0] = ga[:, i * piece : (i + 1) * piece]
+                gsend[i, 1] = gb[:, i * piece : (i + 1) * piece]
+        dp_wait(5 + 2 * step, lambda p: asend.at[step], arecv.at[step])
+        attended = rows_of(arecv.at[step], ndp).astype(BF16)
+        usend[step, :, :width] = jnp.dot(attended, wo_ref[...], preferred_element_type=F32)
+        usend[step, :, width:] = jnp.concatenate(
+            [
+                lax.dot_general(attended, at, NT, preferred_element_type=F32),
+                jnp.zeros((ndp * rolls, 128 - rank), F32),
+            ],
+            axis=1,
+        )
+        tp_start(step, usend.at[step], urecv.at[step])
+        urecv[step, t] = usend[step]
+        if step == 0:
+            src_t = d // half
+            for j in range(per):
+                frm = (d % half) * per + j
+                same = jnp.logical_and(src_t == t, frm == d)
+
+                @pl.when(jnp.logical_not(same))
+                def _():
+                    send(b_ref, bdbuf.at[j], bd_s.at[0], bd_r.at[j], (frm, src_t)).wait_recv()
+
+            bd = lanes_of(bdbuf, per)
+        tp_wait(step, usend.at[step], urecv.at[step])
+        upd = urecv[step, 0]
+        for i in range(1, ntp):
+            upd = upd + urecv[step, i]
+        state = state + (
+            upd[:, :width] + adapter_scale * exact_dot(upd[:, width : width + rank], bd)
+        )
+
+    for i in range(ndp):
+        fsend[i] = state[i * rolls : (i + 1) * rolls]
+    dp_start(8, lambda p: fsend.at[p], frecv)
+    frecv[d] = fsend[d]
+    dp_start(9, lambda p: gsend.at[p], grecv)
+    grecv[d] = gsend[d]
+    line_sends(True)
+    out_ref[...] = adapter_scale * lax.dot_general(low_t, bt, TN, preferred_element_type=F32)
+    xcp.wait_recv()
+    dp_wait(8, lambda p: fsend.at[p], frecv)
+    for i in range(ndp):
+        dec_ref[:, i * width : (i + 1) * width] = frecv[i]
+
+    other_y = 2 * z + (1 - y)
+    other_x = 2 * (1 - x) + c
+
+    def forward(zz, cc, ch):
+        return send(
+            wbuf.at[zz, y, cc, ch],
+            wbuf.at[zz, y, cc, ch],
+            wf_s.at[zz, cc, ch],
+            wf_r.at[zz, cc, ch],
+            (other_y, t),
+        )
+
+    def forwarded(zz, cc, ch):
+        return send(
+            wbuf.at[zz, y, cc, ch],
+            wbuf.at[zz, 1 - y, cc, ch],
+            wf_s.at[zz, cc, ch],
+            wf_r.at[zz, cc, ch],
+            (other_y, t),
+        )
+
+    def share(yy, ch):
+        return send(
+            pbuf.at[yy, ch], prcv.at[yy, ch], ps_s.at[yy, ch], ps_r.at[yy, ch], (d, other_x)
+        )
+
+    def block(zi, zz, yy, ch):
+        p = jnp.dot(xbuf[0], wbuf[zz, yy, 0, ch], preferred_element_type=F32)
+        p = p + jnp.dot(xbuf[1], wbuf[zz, yy, 1, ch], preferred_element_type=F32)
+
+        @pl.when(zi == 0)
+        def _():
+            pbuf[yy, ch] = p
+            share(yy, ch).start()
+
+        @pl.when(zi == 1)
+        def _():
+            cols = pl.ds(pl.multiple_of(yy * chunks * CHUNK + ch * CHUNK, CHUNK), CHUNK)
+            out_ref[:, cols] += p
+
+    def turn(q):
+        zi = q % 2
+        return zi, jnp.where(zi == 0, 1 - x, x), q // 2
+
+    def stage(q, _):
+        @pl.when(q < 2 * chunks)
+        def _():
+            zi, zz, ch = turn(q)
+            for cc in range(2):
+                mine = jnp.logical_and(c + 2 * zz == z, c == cc)
+
+                @pl.when(jnp.logical_not(mine))
+                def _():
+                    send(
+                        wo_ref.at[:, pl.ds(0, CHUNK)],
+                        wbuf.at[zz, y, cc, ch],
+                        wl_s.at[0, 0],
+                        wl_r.at[zz, cc, ch],
+                        (d, mate),
+                    ).wait_recv()
+
+                forward(zz, cc, ch).start()
+            block(zi, zz, y, ch)
+
+        @pl.when(q > 0)
+        def _():
+            zi, zz, ch = turn(q - 1)
+            for cc in range(2):
+                forwarded(zz, cc, ch).wait_recv()
+            block(zi, zz, 1 - y, ch)
+
+        return 0
+
+    lax.fori_loop(0, 2 * chunks + 1, stage, 0)
+
+    dp_wait(9, lambda p: gsend.at[p], grecv)
+    g = grecv[0]
+    for i in range(1, ndp):
+        g = g + grecv[i]
+    ga_ref[...] = g[0]
+    gb_ref[...] = g[1]
+    for yy in range(2):
+        for ch in range(chunks):
+            share(yy, ch).wait_recv()
+            cols = pl.ds((yy * chunks + ch) * CHUNK, CHUNK)
+            out_ref[:, cols] += prcv[yy, ch]
+
+    line_sends(False)
+    for zz in range(2):
+        for cc in range(2):
+            for ch in range(chunks):
+                forward(zz, cc, ch).wait_send()
+    for yy in range(2):
+        for ch in range(chunks):
+            share(yy, ch).wait_send()
+
+    @pl.when(bdst != d)
+    def _():
+        send(b_ref, bdbuf.at[bslot], bd_s.at[0], bd_r.at[bslot], (bdst, t)).wait_send()
+
+    for cp in sent:
+        cp.wait_send()
+
+
+def fused_shards(
+    ndp,
+    ntp,
+    hidden,
+    attention_norm_gain,
+    query_key_value_weight,
+    key_value_cache,
+    cache_fill_lengths,
+    output_weight_frozen,
+    adapter_down_transposed,
+    adapter_up_matrix,
+    attention_rows,
+    upstream,
+    rewards,
+    prompt_group_index,
+    completion_live_lengths,
+):
+    rolls, model = hidden.shape
+    width = model // ndp
+    rank, _, piece = adapter_down_transposed.shape
+    rows, shard = attention_rows.shape
+    qkvw = query_key_value_weight.shape[2]
+    feats = output_weight_frozen.shape[1]
+    chunks = width // CHUNK
+    groups = rolls * ndp // GROUP
+    h = hidden.astype(F32).reshape(rolls, ndp, width).transpose(1, 0, 2)
+    gain = attention_norm_gain.astype(F32).reshape(ndp, 1, width)
+    lane = jnp.arange(128, dtype=jnp.int32)
+    onehot = (prompt_group_index[:, None] == lane[None, :]).astype(F32)
+    spread = lambda v: jnp.broadcast_to(v.astype(F32)[:, None], (rolls, 128))
+    stats = jnp.concatenate(
+        [
+            jnp.sum(onehot * rewards[:, None], axis=0, keepdims=True),
+            jnp.sum(onehot * (rewards * rewards)[:, None], axis=0, keepdims=True),
+            onehot,
+            spread(rewards),
+            spread(completion_live_lengths),
+        ],
+        axis=0,
+    )
+    vm = pl.BlockSpec(memory_space=pltpu.VMEM)
+    sm = pl.BlockSpec(memory_space=pltpu.SMEM)
+    dma = pltpu.SemaphoreType.DMA
+    V = pltpu.VMEM
+    dec, out, ga, gb = pl.pallas_call(
+        lambda *refs: fused_kernel(ndp, ntp, *refs),
+        out_shape=(
+            jax.ShapeDtypeStruct((rolls, model), F32),
+            jax.ShapeDtypeStruct((rows, shard), F32),
+            jax.ShapeDtypeStruct((rank, piece), F32),
+            jax.ShapeDtypeStruct((rank, piece), F32),
+        ),
+        in_specs=[vm, vm, vm, vm, sm, vm, vm, vm, vm, vm, vm],
+        out_specs=(vm, vm, vm, vm),
+        scratch_shapes=[
+            V((ndp, rolls, width), F32),
+            V((ndp, rank, piece), BF16),
+            V((ndp, rank, piece), BF16),
+            V((width // piece, rank, piece), BF16),
+            V((ndp,) + stats.shape, F32),
+            V((2, ndp, rolls, qkvw + 128), F32),
+            V((2, ndp, rolls, qkvw + 128), F32),
+            V((2, rolls, feats), F32),
+            V((2, ndp, rolls, feats), F32),
+            V((2, ndp * rolls, width + 128), F32),
+            V((2, ntp, ndp * rolls, width + 128), F32),
+            V((ndp, rolls, width), F32),
+            V((ndp, rolls, width), F32),
+            V((2, rank, rows), F32),
+            V((ntp, 2, rank, rows), F32),
+            V((ndp, 2, rank, piece), F32),
+            V((ndp, 2, rank, piece), F32),
+            V((rows, shard), BF16),
+            V((2, rows, shard), BF16),
+            V((2, 2, 2, chunks, feats, CHUNK), BF16),
+            V((2, chunks, rows, CHUNK), F32),
+            V((2, chunks, rows, CHUNK), F32),
+            dma((10, ndp)),
+            dma((10, ndp)),
+            dma((3, ntp)),
+            dma((3, ntp)),
+            dma((ntp,)),
+            dma((width // piece,)),
+            dma((1,)),
+            dma((1,)),
+            dma((chunks, ndp // 2)),
+            dma((2, 2, chunks)),
+            dma((2, 2, chunks)),
+            dma((2, 2, chunks)),
+            dma((2, chunks)),
+            dma((2, chunks)),
+            dma((chunks,)),
+        ],
+        compiler_params=pltpu.CompilerParams(
+            collective_id=0, has_side_effects=True, vmem_limit_bytes=60 * 2**20
+        ),
+    )(
+        h,
+        gain,
+        query_key_value_weight[:, 0, :],
+        key_value_cache[:, :, 0, :],
+        cache_fill_lengths,
+        output_weight_frozen[0],
+        adapter_down_transposed[:, 0, :],
+        adapter_up_matrix[:, 0, :],
+        attention_rows,
+        upstream,
+        stats,
+    )
+    return dec, out, ga[:, None, :], gb[:, None, :]
 
 
 def shards(
@@ -170,8 +737,17 @@
         P("dp"),
         P("dp"),
     )
+    ndp, ntp = mesh.shape["dp"], mesh.shape["tp"]
+
+    def body(*args):
+        width = args[5].shape[2]
+        piece = args[6].shape[2]
+        if ntp == 4 and ndp == 8 and piece % 128 == 0 and width % CHUNK == 0:
+            return fused_shards(ndp, ntp, *args)
+        return shards(*args)
+
     return jax.shard_map(
-        shards,
+        body,
         mesh=mesh,
         in_specs=placed,
         out_specs=(P("dp", None), P("dp", "tp"), P(None, "tp", "dp"), P(None, "tp", "dp")),

time: 511 us -> 216 us (0.42)
  the two profiles are of different devices: /device:TPU:0 before, /device:TPU:27 now
where the time goes in v1:
time: 216 us
  Pallas kernels  202 us (94%)
  local copies, waits for them, and re-layouts  7.18 us (3%)
  other arithmetic  5.52 us (3%)
    pallas_call x1, Pallas kernels, fused_shards(): pl.pallas_call(lambda *refs: fused_kernel(ndp, ntp, *refs), out_shape=(ja...  202 us
    unnamed x8, local copies, waits for them, and re-layouts  5.78 us

profile of v1, /device:TPU:27, one launch (start us, length us, event | category | flops | bytes accessed | tf_op | source)
XLA Modules:
  0.0 215.7 jit_solution(3394664327861897377)
XLA Ops:
  0.6 0.7 convert_element_type.9
  1.3 0.1 broadcast_in_dim.12
  1.4 0.7 mul.21
  2.1 0.8 select_reduce_fusion
  2.9 0.7 fusion
  3.6 0.7 mul.19
  4.3 0.6 concatenate.3.refs_10_
  4.9 1.3 reshape.24
  6.2 1.3 convert_bitcast_fusion.refs_0_
  7.6 202.4 %shard_map.156 = (f32[2,4096]{1,0:T(2,128)}, f32[512,1024]{1,0:T(8,128)}, f32[64,128]{1,0:T(8,128)}, f32[64,128]{1,0:T(8,128)}) custom-call(f32[8,2,512]{2,1,0:T(2,128)} %convert_bitcast_fusion.refs_0_, f32[8,1,512]{2,1,0:T(1,128)} %bitcast.21, bf16[512,1280]{1,0:T(8,128)(2,1)} %bitcast.19, bf16[2,2048,256]{2,1,0:T(8,128)(2,1)} %bitcast.18, s32[2]{0:T(128)} %refs_4_.1, ...), custom_call_target="tpu_custom_call" | custom-call | tf_op jit(solution)/shard_map/pallas_call | solution.py:545
  210.0 1.4 copy.23
  211.3 0.0 copy-start.1
  211.3 0.0 copy-start
  211.3 3.2 %copy.24 = f32[512,1024]{1,0:T(8,128)} copy(f32[512,1024]{1,0:T(8,128)} %get-tuple-element.23) | data formatting | bytes 4194304
  214.5 0.0 copy-done.1
  214.5 0.6 copy.25
  215.1 0.0 copy-done
  215.1 0.6 copy.26
Async XLA Ops:
  211.3 3.2 %copy-start.1 = (f32[64,128]{1,0:T(8,128)S(1)}, f32[64,128]{1,0:T(8,128)}, u32[]{:S(2)}) copy-start(f32[64,128]{1,0:T(8,128)} %get-tuple-element.10) | copy-start | bytes 98308
  211.3 3.8 %copy-start = (f32[64,128]{1,0:T(8,128)S(1)}, f32[64,128]{1,0:T(8,128)}, u32[]{:S(2)}) copy-start(f32[64,128]{1,0:T(8,128)} %get-tuple-element.11) | copy-start | bytes 98308

commit v2 on v1

--- a/solution.py
+++ b/solution.py
@@ -51,6 +51,8 @@
 NT = (((1,), (1,)), ((), ()))
 TN = (((0,), (0,)), ((), ()))
 CHUNK = 256
+LINE_PARTS = 8
+ROW_PARTS = 8
 
 
 def split3(v):
@@ -88,11 +90,15 @@
     b_ref,
     x_ref,
     up_ref,
-    stats_ref,
+    rew_ref,
+    idx_ref,
+    live_ref,
     dec_ref,
     out_ref,
     ga_ref,
     gb_ref,
+    hsend,
+    stats_ref,
     hbuf,
     abuf,
     bbuf,
@@ -125,20 +131,16 @@
     xs_r,
     wl_s,
     wl_r,
-    wf_s,
-    wf_r,
     ps_s,
     ps_r,
-    loc,
 ):
     d = lax.axis_index("dp")
     t = lax.axis_index("tp")
     z, y = d // 2, d % 2
     x, c = t // 2, t % 2
     nz = ndp // 2
-    rolls = h_ref.shape[1]
-    width = h_ref.shape[2]
-    model = ndp * width
+    rolls, model = h_ref.shape
+    width = model // ndp
     rank = a_ref.shape[0]
     piece = a_ref.shape[1]
     chunks = wo_ref.shape[1] // CHUNK
@@ -189,8 +191,18 @@
             frm = (t + ntp - off) % ntp
             send(src, dst.at[frm], ts_s.at[e, off], ts_r.at[e, off], (d, frm)).wait_recv()
 
-    dp_start(0, lambda p: h_ref.at[p], hbuf)
-    hbuf[d] = h_ref[d]
+    hidden = h_ref[...].astype(F32)
+    for i in range(ndp):
+        hsend[i] = hidden[:, i * width : (i + 1) * width]
+    lane = lax.broadcasted_iota(jnp.int32, (1, 128), 1)
+    ones = [jnp.where(lane == idx_ref[r], 1.0, 0.0) for r in range(rolls)]
+    stats_ref[...] = jnp.zeros_like(stats_ref)
+    for r in range(rolls):
+        stats_ref[0:1] += ones[r] * rew_ref[r]
+        stats_ref[1:2] += ones[r] * (rew_ref[r] * rew_ref[r])
+
+    dp_start(0, lambda p: hsend.at[p], hbuf)
+    hbuf[d] = hsend[d]
     dp_start(1, lambda p: a_ref, abuf)
     abuf[d] = a_ref[...]
     dp_start(2, lambda p: b_ref, bbuf)
@@ -219,53 +231,70 @@
             cp.start()
             sent.append(cp)
     mate = 2 * x + (1 - c)
-    xcp = send(x_ref, xbuf.at[c], xs_s.at[0], xs_r.at[0], (d, mate))
+    other_y = 2 * z + (1 - y)
+    xcp = send(x_ref, xbuf.at[y, c], xs_s.at[0], xs_r.at[0], (d, mate))
     xcp.start()
     sent.append(xcp)
-    xbuf[c] = x_ref[...]
-
-    dp_wait(0, lambda p: h_ref.at[p], hbuf)
+    xbuf[y, c] = x_ref[...]
+
+    def row_send(k):
+        part = rows // ROW_PARTS
+        seg = pl.ds(k * part, part)
+        send(
+            x_ref.at[seg], xbuf.at[y, c, seg], xs_s.at[1], xs_r.at[1], (other_y, t)
+        ).start()
+
+    def rows_whole():
+        return send(x_ref, xbuf.at[1 - y, c], xs_s.at[1], xs_r.at[1], (other_y, t))
+
+    def relay(dst_core):
+        return send(
+            xbuf.at[1 - y, c], xbuf.at[1 - y, dst_core], xs_s.at[2], xs_r.at[2], (d, mate)
+        )
+
+    def line(ch, off, seg):
+        zt = (z + off) % nz
+        cols = pl.ds(ch * CHUNK, CHUNK)
+        return send(
+            wo_ref.at[seg, cols],
+            wbuf.at[z // 2, c, ch, seg],
+            wl_s.at[ch, off],
+            wl_r.at[z // 2, c, ch],
+            (2 * zt + y, 2 * x + z % 2),
+        )
+
+    def quantum(k):
+        ch, part = k // LINE_PARTS, k % LINE_PARTS
+        size = wo_ref.shape[0] // LINE_PARTS
+        seg = pl.ds(part * size, size)
+        for off in (1, 3, 2):
+            line(ch, off, seg).start()
+
+        @pl.when(z % 2 != c)
+        def _():
+            line(ch, 0, seg).start()
+
+    pending = list(range(chunks * LINE_PARTS))
+    row_parts = list(range(ROW_PARTS))
+
+    def bulk(n, m=0):
+        for _ in range(min(n, len(pending))):
+            quantum(pending.pop(0))
+        for _ in range(min(m, len(row_parts))):
+            row_send(row_parts.pop(0))
+
+    bulk(1, 1)
+
+    @pl.when(z % 2 == c)
+    def _():
+        for ch in range(chunks):
+            wbuf[z // 2, c, ch] = wo_ref[:, ch * CHUNK : (ch + 1) * CHUNK]
+
+    dp_wait(0, lambda p: hsend.at[p], hbuf)
     state = rows_of(hbuf, ndp)
-    gain = gain_ref[d]
+    gain = gain_ref[:, pl.ds(pl.multiple_of(d * width, width), width)].astype(F32)
     new_k, new_v = [], []
     factor = 1.0 / math.sqrt(HD)
-
-    def line_sends(go):
-        for ch in range(chunks):
-            for off in range(nz):
-                zt = (z + off) % nz
-                cp = send(
-                    wo_ref.at[:, pl.ds(ch * CHUNK, CHUNK)],
-                    wbuf.at[z // 2, y, c, ch],
-                    wl_s.at[ch, off],
-                    wl_r.at[z // 2, c, ch],
-                    (2 * zt + y, 2 * x + z % 2),
-                )
-                if off == 0:
-
-                    @pl.when(z % 2 != c)
-                    def _():
-                        if go:
-                            cp.start()
-                        else:
-                            cp.wait_send()
-
-                    if go:
-
-                        @pl.when(z % 2 == c)
-                        def _():
-                            lc = pltpu.make_async_copy(
-                                wo_ref.at[:, pl.ds(ch * CHUNK, CHUNK)],
-                                wbuf.at[z // 2, y, c, ch],
-                                loc.at[ch],
-                            )
-                            lc.start()
-                            lc.wait()
-
-                elif go:
-                    cp.start()
-                else:
-                    cp.wait_send()
 
     for step in range(2):
         squares = jnp.sum(state * state, axis=-1, keepdims=True)
@@ -274,6 +303,7 @@
         for i in range(ndp):
             qsend[step, i] = both[i * rolls : (i + 1) * rolls]
         dp_start(4 + 2 * step, lambda p: qsend.at[step, p], qrecv.at[step])
+        bulk(2, 2)
         qrecv[step, d] = qsend[step, d]
         if step == 0:
             dp_wait(1, lambda p: a_ref, abuf)
@@ -287,9 +317,8 @@
             mean = tot[0:1] / GROUP
             std = jnp.sqrt(jnp.maximum(tot[1:2] / GROUP - mean * mean, 0.09))
             for r in range(rolls):
-                one = stats_ref[2 + r : 3 + r]
-                rew = stats_ref[2 + rolls + r : 3 + rolls + r, 0:1]
-                live = stats_ref[2 + 2 * rolls + r : 3 + 2 * rolls + r, 0:1]
+                one, rew = ones[r], rew_ref[r]
+                live = live_ref[r].astype(F32)
                 adv = (rew - jnp.sum(one * mean, axis=1, keepdims=True)) / jnp.sum(
                     one * std, axis=1, keepdims=True
                 )
@@ -334,6 +363,7 @@
                 [att[h : h + 1] for h in range(HEADS_TP)], axis=1
             )
         dp_start(5 + 2 * step, lambda p: asend.at[step], arecv.at[step])
+        bulk(1, 1)
         arecv[step, d] = asend[step]
         if step == 0:
             tp_start(2, lbsend, lbrecv)
@@ -361,6 +391,7 @@
             axis=1,
         )
         tp_start(step, usend.at[step], urecv.at[step])
+        bulk(1, 1)
         urecv[step, t] = usend[step]
         if step == 0:
             src_t = d // half
@@ -387,61 +418,35 @@
     frecv[d] = fsend[d]
     dp_start(9, lambda p: gsend.at[p], grecv)
     grecv[d] = gsend[d]
-    line_sends(True)
+    bulk(len(pending), len(row_parts))
+    rows_whole().wait_recv()
+    relay(c).start()
     out_ref[...] = adapter_scale * lax.dot_general(low_t, bt, TN, preferred_element_type=F32)
-    xcp.wait_recv()
+    send(x_ref, xbuf.at[y, 1 - c], xs_s.at[0], xs_r.at[0], (d, mate)).wait_recv()
     dp_wait(8, lambda p: fsend.at[p], frecv)
     for i in range(ndp):
         dec_ref[:, i * width : (i + 1) * width] = frecv[i]
-
-    other_y = 2 * z + (1 - y)
-    other_x = 2 * (1 - x) + c
-
-    def forward(zz, cc, ch):
+    relay(1 - c).wait_recv()
+
+    def share(dx, dy, ch):
+        zz = jnp.where(dx == 1, 1 - x, x)
+        yy = jnp.where(dy == 1, 1 - y, y)
         return send(
-            wbuf.at[zz, y, cc, ch],
-            wbuf.at[zz, y, cc, ch],
-            wf_s.at[zz, cc, ch],
-            wf_r.at[zz, cc, ch],
-            (other_y, t),
-        )
-
-    def forwarded(zz, cc, ch):
-        return send(
-            wbuf.at[zz, y, cc, ch],
-            wbuf.at[zz, 1 - y, cc, ch],
-            wf_s.at[zz, cc, ch],
-            wf_r.at[zz, cc, ch],
-            (other_y, t),
-        )
-
-    def share(yy, ch):
-        return send(
-            pbuf.at[yy, ch], prcv.at[yy, ch], ps_s.at[yy, ch], ps_r.at[yy, ch], (d, other_x)
-        )
-
-    def block(zi, zz, yy, ch):
-        p = jnp.dot(xbuf[0], wbuf[zz, yy, 0, ch], preferred_element_type=F32)
-        p = p + jnp.dot(xbuf[1], wbuf[zz, yy, 1, ch], preferred_element_type=F32)
-
-        @pl.when(zi == 0)
+            pbuf.at[dx, dy, ch],
+            prcv.at[dx, dy, ch],
+            ps_s.at[dx, dy, ch],
+            ps_r.at[dx, dy, ch],
+            (2 * z + yy, 2 * zz + c),
+        )
+
+    def stage(q, _):
+        ch, r = q // 4, q % 4
+        dx, dy = 1 - r // 2, 1 - r % 2
+        zz = jnp.where(dx == 1, 1 - x, x)
+        yy = jnp.where(dy == 1, 1 - y, y)
+
+        @pl.when(dy == 1)
         def _():
-            pbuf[yy, ch] = p
-            share(yy, ch).start()
-
-        @pl.when(zi == 1)
-        def _():
-            cols = pl.ds(pl.multiple_of(yy * chunks * CHUNK + ch * CHUNK, CHUNK), CHUNK)
-            out_ref[:, cols] += p
-
-    def turn(q):
-        zi = q % 2
-        return zi, jnp.where(zi == 0, 1 - x, x), q // 2
-
-    def stage(q, _):
-        @pl.when(q < 2 * chunks)
-        def _():
-            zi, zz, ch = turn(q)
             for cc in range(2):
                 mine = jnp.logical_and(c + 2 * zz == z, c == cc)
 
@@ -449,25 +454,29 @@
                 def _():
                     send(
                         wo_ref.at[:, pl.ds(0, CHUNK)],
-                        wbuf.at[zz, y, cc, ch],
+                        wbuf.at[zz, cc, ch],
                         wl_s.at[0, 0],
                         wl_r.at[zz, cc, ch],
                         (d, mate),
                     ).wait_recv()
 
-                forward(zz, cc, ch).start()
-            block(zi, zz, y, ch)
-
-        @pl.when(q > 0)
+        p = jnp.dot(xbuf[yy, 0], wbuf[zz, 0, ch], preferred_element_type=F32)
+        p = p + jnp.dot(xbuf[yy, 1], wbuf[zz, 1, ch], preferred_element_type=F32)
+        last = r == 3
+
+        @pl.when(jnp.logical_not(last))
         def _():
-            zi, zz, ch = turn(q - 1)
-            for cc in range(2):
-                forwarded(zz, cc, ch).wait_recv()
-            block(zi, zz, 1 - y, ch)
+            pbuf[dx, dy, ch] = p
+            share(dx, dy, ch).start()
+
+        @pl.when(last)
+        def _():
+            cols = pl.ds(pl.multiple_of((y * chunks + ch) * CHUNK, CHUNK), CHUNK)
+            out_ref[:, cols] += p
 
         return 0
 
-    lax.fori_loop(0, 2 * chunks + 1, stage, 0)
+    lax.fori_loop(0, 4 * chunks, stage, 0)
 
     dp_wait(9, lambda p: gsend.at[p], grecv)
     g = grecv[0]
@@ -475,20 +484,26 @@
         g = g + grecv[i]
     ga_ref[...] = g[0]
     gb_ref[...] = g[1]
-    for yy in range(2):
-        for ch in range(chunks):
-            share(yy, ch).wait_recv()
-            cols = pl.ds((yy * chunks + ch) * CHUNK, CHUNK)
-            out_ref[:, cols] += prcv[yy, ch]
-
-    line_sends(False)
-    for zz in range(2):
-        for cc in range(2):
-            for ch in range(chunks):
-                forward(zz, cc, ch).wait_send()
-    for yy in range(2):
-        for ch in range(chunks):
-            share(yy, ch).wait_send()
+    for ch in range(chunks):
+        for dx, dy in ((1, 0), (0, 1), (1, 1)):
+            share(dx, dy, ch).wait_recv()
+            yy = (y + dy) % 2
+            cols = pl.ds(pl.multiple_of((yy * chunks + ch) * CHUNK, CHUNK), CHUNK)
+            out_ref[:, cols] += prcv[dx, dy, ch]
+
+    whole = pl.ds(0, wo_ref.shape[0])
+    for ch in range(chunks):
+        for off in range(1, nz):
+            line(ch, off, whole).wait_send()
+
+        @pl.when(z % 2 != c)
+        def _():
+            line(ch, 0, whole).wait_send()
+
+        for dx, dy in ((1, 0), (0, 1), (1, 1)):
+            share(dx, dy, ch).wait_send()
+    rows_whole().wait_send()
+    relay(c).wait_send()
 
     @pl.when(bdst != d)
     def _():
@@ -522,22 +537,6 @@
     qkvw = query_key_value_weight.shape[2]
     feats = output_weight_frozen.shape[1]
     chunks = width // CHUNK
-    groups = rolls * ndp // GROUP
-    h = hidden.astype(F32).reshape(rolls, ndp, width).transpose(1, 0, 2)
-    gain = attention_norm_gain.astype(F32).reshape(ndp, 1, width)
-    lane = jnp.arange(128, dtype=jnp.int32)
-    onehot = (prompt_group_index[:, None] == lane[None, :]).astype(F32)
-    spread = lambda v: jnp.broadcast_to(v.astype(F32)[:, None], (rolls, 128))
-    stats = jnp.concatenate(
-        [
-            jnp.sum(onehot * rewards[:, None], axis=0, keepdims=True),
-            jnp.sum(onehot * (rewards * rewards)[:, None], axis=0, keepdims=True),
-            onehot,
-            spread(rewards),
-            spread(completion_live_lengths),
-        ],
-        axis=0,
-    )
     vm = pl.BlockSpec(memory_space=pltpu.VMEM)
     sm = pl.BlockSpec(memory_space=pltpu.SMEM)
     dma = pltpu.SemaphoreType.DMA
@@ -550,14 +549,16 @@
             jax.ShapeDtypeStruct((rank, piece), F32),
             jax.ShapeDtypeStruct((rank, piece), F32),
         ),
-        in_specs=[vm, vm, vm, vm, sm, vm, vm, vm, vm, vm, vm],
+        in_specs=[vm, vm, vm, vm, sm, vm, vm, vm, vm, vm, sm, sm, sm],
         out_specs=(vm, vm, vm, vm),
         scratch_shapes=[
+            V((ndp, rolls, width), F32),
+            V((8, 128), F32),
             V((ndp, rolls, width), F32),
             V((ndp, rank, piece), BF16),
             V((ndp, rank, piece), BF16),
             V((width // piece, rank, piece), BF16),
-            V((ndp,) + stats.shape, F32),
+            V((ndp, 8, 128), F32),
             V((2, ndp, rolls, qkvw + 128), F32),
             V((2, ndp, rolls, qkvw + 128), F32),
             V((2, rolls, feats), F32),
@@ -571,32 +572,29 @@
             V((ndp, 2, rank, piece), F32),
             V((ndp, 2, rank, piece), F32),
             V((rows, shard), BF16),
-            V((2, rows, shard), BF16),
-            V((2, 2, 2, chunks, feats, CHUNK), BF16),
-            V((2, chunks, rows, CHUNK), F32),
-            V((2, chunks, rows, CHUNK), F32),
+            V((2, 2, rows, shard), BF16),
+            V((2, 2, chunks, feats, CHUNK), BF16),
+            V((2, 2, chunks, rows, CHUNK), F32),
+            V((2, 2, chunks, rows, CHUNK), F32),
             dma((10, ndp)),
             dma((10, ndp)),
             dma((3, ntp)),
             dma((3, ntp)),
             dma((ntp,)),
             dma((width // piece,)),
-            dma((1,)),
-            dma((1,)),
+            dma((3,)),
+            dma((3,)),
             dma((chunks, ndp // 2)),
             dma((2, 2, chunks)),
             dma((2, 2, chunks)),
             dma((2, 2, chunks)),
-            dma((2, chunks)),
-            dma((2, chunks)),
-            dma((chunks,)),
         ],
         compiler_params=pltpu.CompilerParams(
             collective_id=0, has_side_effects=True, vmem_limit_bytes=60 * 2**20
         ),
     )(
-        h,
-        gain,
+        hidden,
+        attention_norm_gain.reshape(1, model),
         query_key_value_weight[:, 0, :],
         key_value_cache[:, :, 0, :],
         cache_fill_lengths,
@@ -605,7 +603,9 @@
         adapter_up_matrix[:, 0, :],
         attention_rows,
         upstream,
-        stats,
+        rewards,
+        prompt_group_index,
+        completion_live_lengths,
     )
     return dec, out, ga[:, None, :], gb[:, None, :]
 

time: 216 us -> 157 us (0.73)
  the two profiles are of different devices: /device:TPU:27 before, /device:TPU:0 now
where the time goes in v2:
time: 157 us
  Pallas kernels  149 us (95%)
  local copies, waits for them, and re-layouts  7.09 us (5%)
    pallas_call x1, Pallas kernels, fused_shards(): pl.pallas_call(lambda *refs: fused_kernel(ndp, ntp, *refs), out_shape=(ja...  149 us
    unnamed x8, local copies, waits for them, and re-layouts  5.78 us

profile of v2, /device:TPU:0, one launch (start us, length us, event | category | flops | bytes accessed | tf_op | source)
XLA Modules:
  0.0 156.9 jit_solution(4473849729174874865)
XLA Ops:
  0.6 1.3 reshape.11.refs_1_
  1.9 149.2 %shard_map.156 = (f32[2,4096]{1,0:T(2,128)}, f32[512,1024]{1,0:T(8,128)}, f32[64,128]{1,0:T(8,128)}, f32[64,128]{1,0:T(8,128)}) custom-call(bf16[2,4096]{1,0:T(2,128)(2,1)} %refs_0_.1, bf16[1,4096]{1,0:T(2,128)(2,1)} %reshape.11.refs_1_, bf16[512,1280]{1,0:T(8,128)(2,1)} %bitcast.12, bf16[2,2048,256]{2,1,0:T(8,128)(2,1)} %bitcast.11, s32[2]{0:T(128)} %refs_4_.1, ...), custom_call_target="tpu_custom_call" | custom-call | tf_op jit(solution)/shard_map/pallas_call | solution.py:544
  151.2 1.4 copy.23
  152.5 0.0 copy-start.1
  152.5 0.0 copy-start
  152.5 3.2 %copy.24 = f32[512,1024]{1,0:T(8,128)} copy(f32[512,1024]{1,0:T(8,128)} %get-tuple-element.21) | data formatting | bytes 4194304
  155.7 0.0 copy-done.1
  155.7 0.6 copy.25
  156.3 0.0 copy-done
  156.3 0.6 copy.26
Async XLA Ops:
  152.5 3.2 %copy-start.1 = (f32[64,128]{1,0:T(8,128)S(1)}, f32[64,128]{1,0:T(8,128)}, u32[]{:S(2)}) copy-start(f32[64,128]{1,0:T(8,128)} %get-tuple-element.10) | copy-start | bytes 98308
  152.5 3.8 %copy-start = (f32[64,128]{1,0:T(8,128)S(1)}, f32[64,128]{1,0:T(8,128)}, u32[]{:S(2)}) copy-start(f32[64,128]{1,0:T(8,128)} %get-tuple-element.11) | copy-start | bytes 98308

commit v3 on v2

--- a/solution.py
+++ b/solution.py
@@ -303,7 +303,7 @@
         for i in range(ndp):
             qsend[step, i] = both[i * rolls : (i + 1) * rolls]
         dp_start(4 + 2 * step, lambda p: qsend.at[step, p], qrecv.at[step])
-        bulk(2, 2)
+        bulk(1, 2)
         qrecv[step, d] = qsend[step, d]
         if step == 0:
             dp_wait(1, lambda p: a_ref, abuf)

time: 157 us -> 157 us (level)
  no operation moved by 1% of the time
where the time goes in v3:
time: 157 us
  Pallas kernels  149 us (95%)
  local copies, waits for them, and re-layouts  7.09 us (5%)
    pallas_call x1, Pallas kernels, fused_shards(): pl.pallas_call(lambda *refs: fused_kernel(ndp, ntp, *refs), out_shape=(ja...  149 us
    unnamed x8, local copies, waits for them, and re-layouts  5.78 us

profile of v3, /device:TPU:0, one launch (start us, length us, event | category | flops | bytes accessed | tf_op | source)
XLA Modules:
  0.0 156.5 jit_solution(2144567989117692435)
XLA Ops:
  0.6 1.3 reshape.11.refs_1_
  1.9 148.8 %shard_map.156 = (f32[2,4096]{1,0:T(2,128)}, f32[512,1024]{1,0:T(8,128)}, f32[64,128]{1,0:T(8,128)}, f32[64,128]{1,0:T(8,128)}) custom-call(bf16[2,4096]{1,0:T(2,128)(2,1)} %refs_0_.1, bf16[1,4096]{1,0:T(2,128)(2,1)} %reshape.11.refs_1_, bf16[512,1280]{1,0:T(8,128)(2,1)} %bitcast.12, bf16[2,2048,256]{2,1,0:T(8,128)(2,1)} %bitcast.11, s32[2]{0:T(128)} %refs_4_.1, ...), custom_call_target="tpu_custom_call" | custom-call | tf_op jit(solution)/shard_map/pallas_call | solution.py:544
  150.8 1.4 copy.23
  152.1 0.0 copy-start.1
  152.1 0.0 copy-start
  152.1 3.2 %copy.24 = f32[512,1024]{1,0:T(8,128)} copy(f32[512,1024]{1,0:T(8,128)} %get-tuple-element.21) | data formatting | bytes 4194304
  155.3 0.0 copy-done.1
  155.3 0.6 copy.25
  155.9 0.0 copy-done
  155.9 0.6 copy.26
Async XLA Ops:
  152.1 3.2 %copy-start.1 = (f32[64,128]{1,0:T(8,128)S(1)}, f32[64,128]{1,0:T(8,128)}, u32[]{:S(2)}) copy-start(f32[64,128]{1,0:T(8,128)} %get-tuple-element.10) | copy-start | bytes 98308
  152.1 3.8 %copy-start = (f32[64,128]{1,0:T(8,128)S(1)}, f32[64,128]{1,0:T(8,128)}, u32[]{:S(2)}) copy-start(f32[64,128]{1,0:T(8,128)} %get-tuple-element.11) | copy-start | bytes 98308
